TPU v7x, 128 devices: a whole 4x4x4 slice. The times are simulated.
128 devices in a mesh: shard: 8 (over y_lo, z), ctx: 8 (over y_hi, x), tp: 2 (over core).
Axes of the slice: x: 4, y: 4 (y_hi: 2, y_lo: 2; y = y_hi * 2 + y_lo), z: 4, core: 2. Of those that a mesh axis runs over, the one named last changes fastest.
Arguments:
- tokens: bfloat16 [8, 2048, 2048], P('shard', 'ctx'), may hold values from -6 to 6
- cotangent: bfloat16 [8, 2048, 2048], P('shard', 'ctx'), may hold values from -6 to 6
- seq_ids: int32 [8, 2048], P('shard'), may hold values from 0 to 1, as said below
- block_ids: int32 [8, 2048], P('shard'), may hold values from 0 to 7, as said below
- keep_layer: int32 [8], P('shard'), may hold values from 0 to 1, as said below
- gain_attn: float32 [2048], replicated, may hold values from 0.25 to 1.75
- gain_ffn: float32 [2048], replicated, may hold values from 0.25 to 1.75
- w_query: float32 [2048, 2048], P('shard', 'tp'), may hold values from -0.125 to 0.125
- w_key: float32 [2048, 512], P('shard', 'tp'), may hold values from -0.125 to 0.125
- w_value: float32 [2048, 512], P('shard', 'tp'), may hold values from -0.125 to 0.125
- w_out: float32 [2048, 2048], P('shard', 'tp'), may hold values from -0.75 to 0.75
- w_gate: float32 [2048, 5632], P('shard', 'tp'), may hold values from -0.125 to 0.125
- w_up: float32 [2048, 5632], P('shard', 'tp'), may hold values from -0.125 to 0.125
- w_down: float32 [2048, 5632], P('shard', 'tp'), may hold values from -0.078125 to 0.078125
Outputs:
- output: bfloat16 [8, 2048, 2048], P('shard', 'ctx')
- input_grad: bfloat16 [8, 2048, 2048], P('shard', 'ctx')
- grad_gain_attn: float32 [2048], P('shard')
- grad_gain_ffn: float32 [2048], P('shard')
- grad_query: float32 [2048, 2048], P('shard', 'tp')
- grad_key: float32 [2048, 512], P('shard', 'tp')
- grad_value: float32 [2048, 512], P('shard', 'tp')
- grad_out: float32 [2048, 2048], P('shard', 'tp')
- grad_gate: float32 [2048, 5632], P('shard', 'tp')
- grad_up: float32 [2048, 5632], P('shard', 'tp')
- grad_down: float32 [2048, 5632], P('shard', 'tp')
Inputs may be any that keep to these rules, and one draw needn't show every extreme that they name: `seq_ids`: each sample holds exactly two documents: id 0 on a leading run of fewer than min(256, 256) positions, id 1 on the rest. Blocks of 256 positions are counted from each document's start: block_ids[p] = (p - start of p's document) // 256. `keep_layer`: at least one sample runs the layer and at least one skips it.
All inputs are finite; a program needn't handle non-finite values.
Results may differ from a plain program's by a relative error of at most 0.02.
Values may be sent and summed in bfloat16 or wider, within the bound.
No kernel may reach another device: no remote copies, remote signals or barrier semaphores. Data moves between devices by JAX's collectives and lax.ppermute only.
A program may use at most 256 MiB of HBM per device.

v0:
```python
import jax
import jax.numpy as jnp
from jax import lax
from jax.sharding import Mesh, PartitionSpec as P

HD = 128
EPS = 1e-05
NEG = -1e30
F32 = jnp.float32
BF16 = jnp.bfloat16
SHARD = ("yl", "z")
SWAP = ((0, 1), (1, 0))


def half(value):
    return value.astype(BF16)


def mm(left, right):
    return jnp.dot(left, right, preferred_element_type=F32)


def mm_nt(left, right):
    return lax.dot_general(left, right, (((1,), (1,)), ((), ())), preferred_element_type=F32)


def mm_tn(left, right):
    return lax.dot_general(left, right, (((0,), (0,)), ((), ())), preferred_element_type=F32)


def swap_cores(value):
    return lax.ppermute(value, "tp", SWAP)


def shift_x(value, hop):
    return lax.ppermute(value, "x", [(i, (i + hop) % 4) for i in range(4)])


def gather_x(value):
    return [value] + [shift_x(value, -hop) for hop in (1, 2, 3)]


def scatter_x(chunks):
    moved = [shift_x(half(chunks[hop]), hop) for hop in (2, 1, 3)]
    return chunks[0] + moved[0].astype(F32) + moved[1].astype(F32) + moved[2].astype(F32)


def absolute(chunks, x_at):
    stacked = jnp.stack(chunks + chunks[:3])
    return lax.dynamic_slice_in_dim(stacked, (4 - x_at) % 4, 4, axis=0)


def rotate(value, cosine, sine):
    turned = jnp.concatenate([-value[..., HD // 2 :], value[..., : HD // 2]], axis=-1)
    return value * cosine + turned * sine


def unrotate(grad, cosine, sine):
    scaled = grad * sine
    return grad * cosine + jnp.concatenate(
        [scaled[..., HD // 2 :], -scaled[..., : HD // 2]], axis=-1
    )


def norm_root(value):
    return lax.rsqrt(jnp.mean(value * value, axis=-1, keepdims=True) + EPS)


def norm_backward(value, root, gain, grad):
    scaled = gain * grad
    grad_value = root * scaled - value * root**3 * jnp.mean(scaled * value, axis=-1, keepdims=True)
    return (grad_value, jnp.sum(grad * value * root, axis=0))


def per_device(
    tokens,
    cotangent,
    seq_ids,
    block_ids,
    keep_layer,
    gain_attn,
    gain_ffn,
    w_query,
    w_key,
    w_value,
    w_out,
    w_gate,
    w_up,
    w_down,
):
    core, x_at, y_at = (lax.axis_index("tp"), lax.axis_index("x"), lax.axis_index("yh"))
    first = core == 0
    rows = tokens.shape[1] // 2
    width = tokens.shape[2]
    keep = keep_layer[0].astype(F32)
    scale = HD ** (-0.5)
    side = x_at // 2
    at = x_at % 2
    wq = half(lax.dynamic_slice_in_dim(w_query, at * 512, 512, axis=1))
    wk = half(lax.dynamic_slice_in_dim(w_key, at * HD, HD, axis=1))
    wv = half(lax.dynamic_slice_in_dim(w_value, at * HD, HD, axis=1))
    wo = half(lax.dynamic_slice_in_dim(w_out, at * 512, 512, axis=1))
    pack0 = jnp.concatenate([wq[:, :256], wk, wo[:, :256]], axis=1)
    pack1 = jnp.concatenate([wq[:, 256:], wv, wo[:, 256:]], axis=1)
    lent = lax.ppermute(
        jnp.where(first, pack1, pack0),
        ("x", "tp"),
        [(2 * i + i // 2, 2 * i + 1 - i // 2) for i in range(4)],
    )
    pack = jnp.where(core == side, jnp.where(first, pack0, pack1), lent)
    pack = lax.all_gather(pack, SHARD, axis=0, tiled=True)
    pack_other = swap_cores(pack)
    att0 = jnp.where(first, pack, pack_other)
    att1 = jnp.where(first, pack_other, pack)
    full_qkv = jnp.concatenate([att0[:, :384], att1[:, :384]], axis=1)
    full_out = jnp.concatenate([att0[:, 384:], att1[:, 384:]], axis=1)
    units = w_gate.shape[1] // 4

    def hidden_units(weight):
        own = half(lax.dynamic_slice_in_dim(weight, x_at * units, units, axis=1))
        own = lax.all_gather(own, SHARD, axis=0, tiled=True)
        return (own, swap_cores(own))

    xval = lax.dynamic_slice_in_dim(tokens[0], core * rows, rows, axis=0).astype(F32)
    grad_top = lax.dynamic_slice_in_dim(cotangent[0], core * rows, rows, axis=0).astype(F32)
    root_attn = norm_root(xval)
    normed_attn = jnp.concatenate(gather_x(half(xval * root_attn * gain_attn)), axis=0)
    count = normed_attn.shape[0]

    def of_positions(line, y_index, core_index):
        grid = line.reshape(2, 4, 2, rows)
        picked = lax.dynamic_index_in_dim(grid, y_index, 0, keepdims=False)
        picked = lax.dynamic_index_in_dim(picked, core_index, 1, keepdims=False)
        double = jnp.concatenate([picked, picked], axis=0)
        return lax.dynamic_slice_in_dim(double, x_at, 4, axis=0).reshape(-1)

    corners = ((y_at, core), (y_at, 1 - core), (1 - y_at, core), (1 - y_at, 1 - core))
    seg_query = of_positions(seq_ids[0], y_at, core)
    blk_query = of_positions(block_ids[0], y_at, core)
    seg_keys = jnp.concatenate([of_positions(seq_ids[0], *corner) for corner in corners])
    blk_keys = jnp.concatenate([of_positions(block_ids[0], *corner) for corner in corners])
    allowed = (seg_query[:, None] == seg_keys[None, :]) & (blk_keys[None, :] <= blk_query[:, None])
    position = of_positions(jnp.arange(seq_ids.shape[1], dtype=jnp.int32), y_at, core)
    freqs = 10000.0 ** (-(jnp.arange(HD // 2).astype(F32) * 2.0 / HD))
    angle = position.astype(F32)[:, None] * freqs[None, :]
    cosine = jnp.concatenate([jnp.cos(angle), jnp.cos(angle)], axis=-1)
    sine = jnp.concatenate([jnp.sin(angle), jnp.sin(angle)], axis=-1)
    qkv = mm(normed_attn, full_qkv)
    starts = (0, 128, 384, 512)
    query = jnp.stack([half(rotate(qkv[:, s : s + HD], cosine, sine)) for s in starts])
    keys_values = jnp.concatenate(
        [half(rotate(qkv[:, 256:384], cosine, sine)), half(qkv[:, 640:])], axis=1
    )

    def across_y(value):
        return lax.ppermute(value, "yh", SWAP)

    two_kv = jnp.concatenate([keys_values, across_y(keys_values)], axis=0)
    other_kv = swap_cores(two_kv)
    all_kv = jnp.concatenate(
        [two_kv[:count], other_kv[:count], two_kv[count:], other_kv[count:]], axis=0
    )
    all_keys, all_values = (all_kv[:, :HD], all_kv[:, HD:])
    raw = jnp.einsum("htd,nd->htn", query, all_keys, preferred_element_type=F32) * scale
    safe = jnp.where(allowed[None], raw, NEG)
    top = jnp.max(safe, axis=-1, keepdims=True)
    weights = jnp.where(allowed[None], jnp.exp(safe - top), 0.0)
    total = jnp.sum(weights, axis=-1, keepdims=True)
    added = jnp.einsum("htn,nd->htd", half(weights), all_values, preferred_element_type=F32)
    heads_f = added / total
    log_total = top + jnp.log(total)
    heads = half(heads_f.transpose(1, 0, 2).reshape(count, 4 * HD))

    def chunked(value):
        return [value[j * rows : (j + 1) * rows] for j in range(4)]

    attn_branch = scatter_x(chunked(mm_nt(heads, full_out)))
    middle = xval + keep * attn_branch
    root_ffn = norm_root(middle)
    normed_ffn = jnp.concatenate(gather_x(half(middle * root_ffn * gain_ffn)), axis=0)
    full_gate, full_up, full_down = (hidden_units(w_gate), hidden_units(w_up), hidden_units(w_down))
    d_ffn = jnp.concatenate(gather_x(half(keep * grad_top)), axis=0)
    branch = 0.0
    d_normed = 0.0
    grads_gate, grads_up, grads_down = ([], [], [])
    for wg, wu, wd in zip(full_gate, full_up, full_down, strict=True):
        gate = mm(normed_ffn, wg)
        up = mm(normed_ffn, wu)
        sig = jax.nn.sigmoid(gate)
        silu = gate * sig
        hidden = half(silu * up)
        branch = branch + mm_nt(hidden, wd)
        d_hidden = mm(d_ffn, wd)
        d_gate = half(d_hidden * up * sig * (1.0 + gate * (1.0 - sig)))
        d_up = half(d_hidden * silu)
        d_normed = d_normed + mm_nt(d_gate, wg) + mm_nt(d_up, wu)
        grads_gate.append(mm_tn(normed_ffn, d_gate))
        grads_up.append(mm_tn(normed_ffn, d_up))
        grads_down.append(mm_tn(d_ffn, hidden))
    d_normed_ffn = scatter_x(chunked(d_normed))
    ffn_branch = scatter_x(chunked(branch))

    def both_cores(value):
        other = swap_cores(value)
        return jnp.concatenate(
            [jnp.where(first, value, other), jnp.where(first, other, value)], axis=0
        )

    output = both_cores(half(middle + keep * ffn_branch))

    def reduce_columns(mine, theirs):
        value = half(mine + swap_cores(half(theirs)).astype(F32))
        value = lax.psum_scatter(value, SHARD, scatter_dimension=0, tiled=True)
        value = half(value.astype(F32) + across_y(value).astype(F32))
        return absolute(gather_x(value), x_at)

    def units_of(value):
        return jnp.concatenate([value[i] for i in range(4)], axis=1).astype(F32)

    grad_down = units_of(reduce_columns(*grads_down))
    grad_gate = units_of(reduce_columns(*grads_gate))
    grad_up = units_of(reduce_columns(*grads_up))
    mid_part, gain_ffn_local = norm_backward(middle, root_ffn, gain_ffn, d_normed_ffn)
    d_middle = grad_top + mid_part
    d_attn = jnp.concatenate(gather_x(half(keep * d_middle)), axis=0)
    d_heads = half(mm(d_attn, full_out))
    d_heads_g = d_heads.reshape(count, 4, HD).transpose(1, 0, 2)
    row_delta = jnp.sum(d_heads_g.astype(F32) * heads_f, axis=-1, keepdims=True)
    raw = jnp.einsum("htd,nd->htn", query, all_keys, preferred_element_type=F32) * scale
    probs = jnp.where(allowed[None], jnp.exp(raw - log_total), 0.0)
    d_probs = jnp.einsum("htd,nd->htn", d_heads_g, all_values, preferred_element_type=F32)
    d_scores = half(scale * probs * (d_probs - row_delta))
    grad_q = jnp.einsum("htn,nd->htd", d_scores, all_keys, preferred_element_type=F32)
    key_part = jnp.einsum("htn,htd->nd", d_scores, query, preferred_element_type=F32)
    value_part = jnp.einsum("htn,htd->nd", half(probs), d_heads_g, preferred_element_type=F32)
    kv_part = jnp.concatenate([key_part, value_part], axis=1)
    kv_mine = jnp.concatenate([kv_part[:count], kv_part[2 * count : 3 * count]], axis=0)
    kv_theirs = jnp.concatenate([kv_part[count : 2 * count], kv_part[3 * count :]], axis=0)
    kv_two = kv_mine + swap_cores(half(kv_theirs)).astype(F32)
    grad_kv = kv_two[:count] + across_y(half(kv_two[count:])).astype(F32)
    d_q = [half(unrotate(grad_q[h], cosine, sine)) for h in range(4)]
    d_key = half(unrotate(grad_kv[:, :HD], cosine, sine))
    d_qkv = jnp.concatenate([d_q[0], d_q[1], d_key, d_q[2], d_q[3], half(grad_kv[:, HD:])], axis=1)
    d_normed_attn = scatter_x(chunked(mm_nt(d_qkv, full_qkv)))
    grad_qkv = mm_tn(normed_attn, d_qkv)
    grad_o = mm_tn(d_attn, heads)
    grads0 = jnp.concatenate([grad_qkv[:, :384], grad_o[:, :256]], axis=1)
    grads1 = jnp.concatenate([grad_qkv[:, 384:], grad_o[:, 256:]], axis=1)
    packs = reduce_columns(jnp.where(first, grads0, grads1), jnp.where(first, grads1, grads0))
    mine = lax.dynamic_slice_in_dim(packs, 2 * core, 2, axis=0)
    theirs = swap_cores(lax.dynamic_slice_in_dim(packs, 2 - 2 * core, 2, axis=0))
    out0 = jnp.where(first, mine, theirs).astype(F32)
    out1 = jnp.where(first, theirs, mine).astype(F32)
    grad_query = jnp.concatenate(
        [out0[0, :, :256], out1[0, :, :256], out0[1, :, :256], out1[1, :, :256]], axis=1
    )
    grad_key = jnp.concatenate([out0[0, :, 256:384], out0[1, :, 256:384]], axis=1)
    grad_value = jnp.concatenate([out1[0, :, 256:384], out1[1, :, 256:384]], axis=1)
    grad_out = jnp.concatenate(
        [out0[0, :, 384:], out1[0, :, 384:], out0[1, :, 384:], out1[1, :, 384:]], axis=1
    )
    input_part, gain_attn_local = norm_backward(xval, root_attn, gain_attn, d_normed_attn)
    input_grad = both_cores(half(d_middle + input_part))
    gains = lax.psum(jnp.stack([gain_attn_local, gain_ffn_local]), ("yl", "z", "yh", "x", "tp"))
    owned = width // 8
    gains = lax.dynamic_slice_in_dim(
        gains, (lax.axis_index("yl") * 4 + lax.axis_index("z")) * owned, owned, axis=1
    )
    return (
        output[None],
        input_grad[None],
        gains[0],
        gains[1],
        grad_query,
        grad_key,
        grad_value,
        grad_out,
        grad_gate,
        grad_up,
        grad_down,
    )


def solution(mesh):
    fine = Mesh(mesh.devices.reshape(2, 4, 2, 4, 2), ("yl", "z", "yh", "x", "tp"))
    shard, ctx = (("yl", "z"), ("yh", "x"))
    acts, weight = (P(shard, ctx, None), P(shard, "tp"))
    return jax.shard_map(
        per_device,
        mesh=fine,
        in_specs=(acts, acts, P(shard, None), P(shard, None), P(shard), P(), P()) + (weight,) * 7,
        out_specs=(acts, acts, P(shard), P(shard)) + (weight,) * 7,
        check_vma=False,
    )
```

profile of v0, /device:TPU:17, one launch (start us, length us, event | category | flops | bytes accessed | tf_op | source)
XLA Modules:
  0.0 724.8 jit_solution(15446372410941713195)
XLA Ops:
  25.9 42.6 %all-gather.5.cloned.1.call-done = bf16[2048,640]{0,1:T(8,128)(2,1)} async-done(((bf16[256,640]{0,1:T(8,128)(2,1)}), bf16[2048,640]{0,1:T(8,128)(2,1)}) %all-gather.5.cloned.1.call-update) | async-done | bytes 2621456 | tf_op jit(solution)/shard_map/all_gather | solution.py:111
  89.1 12.2 %collective-permute-done.1 = bf16[128,2048]{1,0:T(8,128)(2,1)} collective-permute-done((bf16[128,2048]{1,0:T(8,128)(2,1)}, bf16[128,2048]{1,0:T(8,128)(2,1)}, u32[]{:S(2)}, u32[]{:S(2)}) %collective-permute-start.1) | collective-permute-done | bytes 524320 | tf_op jit(solution)/shard_map/ppermute | solution.py:36
  108.0 12.4 %collective-permute-done.5 = bf16[512,256]{1,0:T(8,128)(2,1)S(1)} collective-permute-done((bf16[512,256]{1,0:T(8,128)(2,1)S(1)}, bf16[512,256]{1,0:T(8,128)(2,1)S(1)}, u32[]{:S(2)}, u32[]{:S(2)}) %collective-permute-start.5) | collective-permute-done | bytes 262176 | tf_op jit(solution)/shard_map/ppermute | solution.py:156
  126.9 5.1 collective-permute-start.15
  132.0 48.6 %all-gather.9.cloned.1.call-done = bf16[2048,704]{0,1:T(8,128)(2,1)} async-done(((bf16[256,704]{0,1:T(8,128)(2,1)}), bf16[2048,704]{0,1:T(8,128)(2,1)}) %all-gather.9.cloned.1.call-update) | async-done | bytes 2883600 | tf_op jit(solution)/shard_map/all_gather | solution.py:121
  180.6 4.9 collective-permute-start.14
  196.5 5.0 fusion.1
  202.3 5.7 fusion.43
  214.9 19.1 %all-gather.7.cloned.1.call-done = bf16[2048,704]{0,1:T(8,128)(2,1)} async-done(((bf16[256,704]{0,1:T(8,128)(2,1)}), bf16[2048,704]{0,1:T(8,128)(2,1)}) %all-gather.7.cloned.1.call-update) | async-done | bytes 2883600 | tf_op jit(solution)/shard_map/all_gather | solution.py:121
  234.0 5.0 collective-permute-start.13
  243.6 10.8 %collective-permute-done.7 = bf16[128,2048]{1,0:T(8,128)(2,1)} collective-permute-done((bf16[128,2048]{1,0:T(8,128)(2,1)}, bf16[128,2048]{1,0:T(8,128)(2,1)}, u32[]{:S(2)}, u32[]{:S(2)}) %collective-permute-start.7) | collective-permute-done | bytes 524320 | tf_op jit(solution)/shard_map/ppermute | solution.py:36
  259.2 6.9 collective-permute-done.22
  266.8 10.0 %collective-permute-done.21 = bf16[128,2048]{1,0:T(8,128)(2,1)S(1)} collective-permute-done((bf16[128,2048]{1,0:T(8,128)(2,1)}, bf16[128,2048]{1,0:T(8,128)(2,1)S(1)}, u32[]{:S(2)}, u32[]{:S(2)}) %collective-permute-start.21) | collective-permute-done | bytes 524320 | tf_op jit(solution)/shard_map/ppermute | solution.py:36
  290.6 11.6 %collective-permute-done.11 = bf16[128,2048]{1,0:T(8,128)(2,1)S(1)} collective-permute-done((bf16[128,2048]{1,0:T(8,128)(2,1)S(1)}, bf16[128,2048]{1,0:T(8,128)(2,1)S(1)}, u32[]{:S(2)}, u32[]{:S(2)}) %collective-permute-start.11) | collective-permute-done | bytes 524320 | tf_op jit(solution)/shard_map/ppermute | solution.py:36
  302.2 4.7 collective-permute-done.10
  344.4 5.8 fusion.130
  352.8 11.0 %collective-permute-done.25 = bf16[128,2048]{1,0:T(8,128)(2,1)S(1)} collective-permute-done((bf16[128,2048]{1,0:T(8,128)(2,1)S(1)}, bf16[128,2048]{1,0:T(8,128)(2,1)S(1)}, u32[]{:S(2)}, u32[]{:S(2)}) %collective-permute-start.25) | collective-permute-done | bytes 524320 | tf_op jit(solution)/shard_map/ppermute | solution.py:36
  374.3 12.0 %collective-permute-done.18 = bf16[128,2048]{1,0:T(8,128)(2,1)S(1)} collective-permute-done((bf16[128,2048]{1,0:T(8,128)(2,1)}, bf16[128,2048]{1,0:T(8,128)(2,1)S(1)}, u32[]{:S(2)}, u32[]{:S(2)}) %collective-permute-start.18) | collective-permute-done | bytes 524320 | tf_op jit(solution)/shard_map/ppermute | solution.py:36
  408.5 14.0 %collective-permute-start.19 = (bf16[128,2048]{1,0:T(8,128)(2,1)}, bf16[128,2048]{1,0:T(8,128)(2,1)}, u32[]{:S(2)}, u32[]{:S(2)}) collective-permute-start(bf16[128,2048]{1,0:T(8,128)(2,1)} %get-tuple-element.127), channel_id=1, source_target_pairs={{0,1},{1,0},{2,3},{3,2},{4,5},{5,4},{6,7},{7,6},{8,9},{9,8},{10,11... | collective-permute-start | bytes 1572872 | tf_op jit(solution)/shard_map/ppermute | solution.py:32
  424.4 12.5 %multiply_convert_fusion = bf16[4,512,2048]{2,1,0:T(8,128)(2,1)} fusion(f32[4,512,2048]{2,1,0:T(8,128)} %copy-done.5, f32[4,512]{1,0:T(4,128)S(1)} %get-tuple-element.171, f32[4,512]{1,0:T(4,128)S(1)} %log_add_fusion, pred[512,2048]{1,0:T(8,128)(4,1)S(1)} %copy-done.13, bf16[4,512,128]{1,2,0:T(8,128)(2,1)S(1)} %bitcast.246, bf16[2048,256]{1,0:T(8,128)(2,1)S(1)} %copy-done.31), kind=kOutput, calls=%fused_computation | convolution fusion | flops 1103101952 | bytes 27279360 | tf_op jit(solution)/shard_map/htd,nd->htn/dot_general | solution.py:231
  436.9 5.8 convolution_bitcast_fusion
  442.8 8.1 %fusion.9 = f32[2048,128]{1,0:T(8,128)S(1)} fusion(bf16[4,512,128]{1,2,0:T(8,128)(2,1)S(1)} %bitcast.247, f32[4,512,2048]{2,1,0:T(8,128)} %copy-done.5, f32[4,512]{1,0:T(4,128)S(1)} %log_add_fusion, pred[512,2048]{1,0:T(8,128)(4,1)S(1)} %copy-done.13), kind=kOutput, calls=%fused_computation.33 | convolution fusion | flops 1090519040 | bytes 19406848 | tf_op jit(solution)/shard_map/htn,htd->nd/dot_general | solution.py:235
  465.5 10.9 %collective-permute-done.30 = bf16[512,256]{1,0:T(8,128)(2,1)S(1)} collective-permute-done((bf16[512,256]{1,0:T(8,128)(2,1)S(1)}, bf16[512,256]{1,0:T(8,128)(2,1)S(1)}, u32[]{:S(2)}, u32[]{:S(2)}) %collective-permute-start.30) | collective-permute-done | bytes 262176 | tf_op jit(solution)/shard_map/ppermute | solution.py:156
  479.4 5.5 add_convert_fusion
  507.5 9.2 %collective-permute-done.31 = bf16[128,2048]{1,0:T(8,128)(2,1)S(1)} collective-permute-done((bf16[128,2048]{1,0:T(8,128)(2,1)S(1)}, bf16[128,2048]{1,0:T(8,128)(2,1)S(1)}, u32[]{:S(2)}, u32[]{:S(2)}) %collective-permute-start.31) | collective-permute-done | bytes 524320 | tf_op jit(solution)/shard_map/ppermute | solution.py:36
  522.6 70.6 %psum.7 = f32[2,2048]{1,0:T(2,128)S(1)} all-reduce(f32[2,2048]{1,0:T(2,128)S(1)} %pad_maximum_fusion.34), channel_id=1, replica_groups=mesh['yl'=2,'z'=4,'yh'=2,'x'=4,'tp'=2] {'yl','z','yh','x','tp'}, use_global_device_ids=true, to_apply=%region_9.10 | all-reduce | flops 4096 | bytes 32768 | tf_op jit(solution)/shard_map/psum | solution.py:264
  596.6 5.7 add_convert_fusion.3
  610.1 8.0 %collective-permute-done.47 = bf16[256,704]{0,1:T(8,128)(2,1)S(1)} collective-permute-done((bf16[256,704]{0,1:T(8,128)(2,1)}, bf16[256,704]{0,1:T(8,128)(2,1)S(1)}, u32[]{:S(2)}, u32[]{:S(2)}) %collective-permute-start.47) | collective-permute-done | bytes 360480 | tf_op jit(solution)/shard_map/ppermute | solution.py:156
  618.2 14.8 %collective-permute-done.52 = bf16[256,704]{0,1:T(8,128)(2,1)S(1)} collective-permute-done((bf16[256,704]{0,1:T(8,128)(2,1)}, bf16[256,704]{0,1:T(8,128)(2,1)S(1)}, u32[]{:S(2)}, u32[]{:S(2)}) %collective-permute-start.52) | collective-permute-done | bytes 360480 | tf_op jit(solution)/shard_map/ppermute | solution.py:156
  640.9 14.2 %collective-permute-done.50 = bf16[256,704]{0,1:T(8,128)(2,1)S(1)} collective-permute-done((bf16[256,704]{0,1:T(8,128)(2,1)S(1)}, bf16[256,704]{0,1:T(8,128)(2,1)S(1)}, u32[]{:S(2)}, u32[]{:S(2)}) %collective-permute-start.50) | collective-permute-done | bytes 360480 | tf_op jit(solution)/shard_map/ppermute | solution.py:36
  659.8 7.6 %collective-permute-done.55 = bf16[256,704]{0,1:T(8,128)(2,1)} collective-permute-done((bf16[256,704]{0,1:T(8,128)(2,1)}, bf16[256,704]{0,1:T(8,128)(2,1)}, u32[]{:S(2)}, u32[]{:S(2)}) %collective-permute-start.55) | collective-permute-done | bytes 360480 | tf_op jit(solution)/shard_map/ppermute | solution.py:36
  680.9 9.2 %collective-permute-done.39 = bf16[256,640]{0,1:T(8,128)(2,1)S(1)} collective-permute-done((bf16[256,640]{0,1:T(8,128)(2,1)S(1)}, bf16[256,640]{0,1:T(8,128)(2,1)S(1)}, u32[]{:S(2)}, u32[]{:S(2)}) %collective-permute-start.39) | collective-permute-done | bytes 327712 | tf_op jit(solution)/shard_map/ppermute | solution.py:36
  (478 shorter events, 278.1 us)
Async XLA Ops:
  7.2 61.2 %all-gather.5.cloned.1.call-start = ((), (), s32[]{:S(2)}) async-start(), calls=%async_computation.4 | async-start | bytes 2949120 | tf_op jit(solution)/shard_map/all_gather | solution.py:111
  21.5 105.4 %all-gather.11.cloned.1.call-start = ((), (), s32[]{:S(2)}) async-start(), calls=%async_computation.7 | async-start | bytes 3244032 | tf_op jit(solution)/shard_map/all_gather | solution.py:121
  22.7 157.9 %all-gather.9.cloned.1.call-start = ((), (), s32[]{:S(2)}) async-start(), calls=%async_computation.6 | async-start | bytes 3244032 | tf_op jit(solution)/shard_map/all_gather | solution.py:121
  25.1 208.9 %all-gather.7.cloned.1.call-start = ((), (), s32[]{:S(2)}) async-start(), calls=%async_computation.5 | async-start | bytes 3244032 | tf_op jit(solution)/shard_map/all_gather | solution.py:121
  75.3 26.0 %collective-permute-start.1 = (bf16[128,2048]{1,0:T(8,128)(2,1)}, bf16[128,2048]{1,0:T(8,128)(2,1)}, u32[]{:S(2)}, u32[]{:S(2)}) collective-permute-start(bf16[128,2048]{1,0:T(8,128)(2,1)} %fusion.23), channel_id=1, source_target_pairs={{0,4},{2,6},{4,0},{6,2},{1,5},{3,7},{5,1},{7,3},{8,12},{10,14},{12... | collective-permute-start | bytes 1572872 | tf_op jit(solution)/shard_map/ppermute | solution.py:36
  81.1 515.0 %reduce-scatter.7.cloned.1.call-start = ((), (), s32[]{:S(2)}) async-start(), calls=%async_computation.9 | async-start | bytes 3244032 | tf_op jit(solution)/shard_map/reduce_scatter | solution.py:213
  121.3 70.3 %collective-permute-start.6 = (bf16[1024,256]{1,0:T(8,128)(2,1)}, bf16[1024,256]{1,0:T(8,128)(2,1)}, u32[]{:S(2)}, u32[]{:S(2)}) collective-permute-start(bf16[1024,256]{1,0:T(8,128)(2,1)} %pad_maximum_fusion.19), channel_id=1, source_target_pairs={{0,1},{1,0},{2,3},{3,2},{4,5},{5,4},{6,7},{7,6},{8,9},{9,8},{10,11... | collective-permute-start | bytes 1572872 | tf_op jit(solution)/shard_map/ppermute | solution.py:32
  126.9 155.7 %collective-permute-start.15 = (bf16[2048,704]{0,1:T(8,128)(2,1)}, bf16[2048,704]{0,1:T(8,128)(2,1)}, u32[]{:S(2)}, u32[]{:S(2)}) collective-permute-start(bf16[2048,704]{0,1:T(8,128)(2,1)} %all-gather.11.cloned.1.call-done), channel_id=1, source_target_pairs={{0,1},{1,0},{2,3},{3,2},{4,5},{5,4},{6,7},{7,6},{8,9},{9,8},{10,11... | collective-permute-start | bytes 8650760 | tf_op jit(solution)/shard_map/ppermute | solution.py:32
  180.6 107.6 %collective-permute-start.14 = (bf16[2048,704]{0,1:T(8,128)(2,1)}, bf16[2048,704]{0,1:T(8,128)(2,1)}, u32[]{:S(2)}, u32[]{:S(2)}) collective-permute-start(bf16[2048,704]{0,1:T(8,128)(2,1)} %all-gather.9.cloned.1.call-done), channel_id=1, source_target_pairs={{0,1},{1,0},{2,3},{3,2},{4,5},{5,4},{6,7},{7,6},{8,9},{9,8},{10,11... | collective-permute-start | bytes 8650760 | tf_op jit(solution)/shard_map/ppermute | solution.py:32
  212.5 26.5 %collective-permute-start.9 = (bf16[128,2048]{1,0:T(8,128)(2,1)}, bf16[128,2048]{1,0:T(8,128)(2,1)S(1)}, u32[]{:S(2)}, u32[]{:S(2)}) collective-permute-start(bf16[128,2048]{1,0:T(8,128)(2,1)} %get-tuple-element.91), channel_id=1, source_target_pairs={{0,6},{2,0},{4,2},{6,4},{1,7},{3,1},{5,3},{7,5},{8,14},{10,8},{12,... | collective-permute-start | bytes 1572872 | tf_op jit(solution)/shard_map/ppermute | solution.py:36
  214.9 28.3 %collective-permute-start.8 = (bf16[128,2048]{1,0:T(8,128)(2,1)}, bf16[128,2048]{1,0:T(8,128)(2,1)}, u32[]{:S(2)}, u32[]{:S(2)}) collective-permute-start(bf16[128,2048]{1,0:T(8,128)(2,1)} %get-tuple-element.92), channel_id=1, source_target_pairs={{0,2},{2,4},{4,6},{6,0},{1,3},{3,5},{5,7},{7,1},{8,10},{10,12},{12... | collective-permute-start | bytes 1572872 | tf_op jit(solution)/shard_map/ppermute | solution.py:36
  234.0 76.7 %collective-permute-start.13 = (bf16[2048,704]{0,1:T(8,128)(2,1)}, bf16[2048,704]{0,1:T(8,128)(2,1)}, u32[]{:S(2)}, u32[]{:S(2)}) collective-permute-start(bf16[2048,704]{0,1:T(8,128)(2,1)} %all-gather.7.cloned.1.call-done), channel_id=1, source_target_pairs={{0,1},{1,0},{2,3},{3,2},{4,5},{5,4},{6,7},{7,6},{8,9},{9,8},{10,11... | collective-permute-start | bytes 8650760 | tf_op jit(solution)/shard_map/ppermute | solution.py:32
  318.1 51.7 %collective-permute-start.41 = (bf16[2048,704]{0,1:T(8,128)(2,1)}, bf16[2048,704]{0,1:T(8,128)(2,1)}, u32[]{:S(2)}, u32[]{:S(2)}) collective-permute-start(bf16[2048,704]{0,1:T(8,128)(2,1)} %convolution_convert_fusion.2), channel_id=1, source_target_pairs={{0,1},{1,0},{2,3},{3,2},{4,5},{5,4},{6,7},{7,6},{8,9},{9,8},{10,11... | collective-permute-start | bytes 8650760 | tf_op jit(solution)/shard_map/ppermute | solution.py:32
  338.4 25.3 %collective-permute-start.25 = (bf16[128,2048]{1,0:T(8,128)(2,1)S(1)}, bf16[128,2048]{1,0:T(8,128)(2,1)S(1)}, u32[]{:S(2)}, u32[]{:S(2)}) collective-permute-start(bf16[128,2048]{1,0:T(8,128)(2,1)S(1)} %get-tuple-element.85), channel_id=1, source_target_pairs={{0,6},{2,0},{4,2},{6,4},{1,7},{3,1},{5,3},{7,5},{8,14},{10,8},{12,... | collective-permute-start | bytes 1572872 | tf_op jit(solution)/shard_map/ppermute | solution.py:36
  341.3 25.7 %collective-permute-start.24 = (bf16[128,2048]{1,0:T(8,128)(2,1)S(1)}, bf16[128,2048]{1,0:T(8,128)(2,1)S(1)}, u32[]{:S(2)}, u32[]{:S(2)}) collective-permute-start(bf16[128,2048]{1,0:T(8,128)(2,1)S(1)} %get-tuple-element.86), channel_id=1, source_target_pairs={{0,2},{2,4},{4,6},{6,0},{1,3},{3,5},{5,7},{7,1},{8,10},{10,12},{12... | collective-permute-start | bytes 1572872 | tf_op jit(solution)/shard_map/ppermute | solution.py:36
  341.3 27.2 %collective-permute-start.23 = (bf16[128,2048]{1,0:T(8,128)(2,1)S(1)}, bf16[128,2048]{1,0:T(8,128)(2,1)S(1)}, u32[]{:S(2)}, u32[]{:S(2)}) collective-permute-start(bf16[128,2048]{1,0:T(8,128)(2,1)S(1)} %get-tuple-element.84), channel_id=1, source_target_pairs={{0,4},{2,6},{4,0},{6,2},{1,5},{3,7},{5,1},{7,3},{8,12},{10,14},{12... | collective-permute-start | bytes 1572872 | tf_op jit(solution)/shard_map/ppermute | solution.py:36
  351.4 35.0 %collective-permute-start.18 = (bf16[128,2048]{1,0:T(8,128)(2,1)}, bf16[128,2048]{1,0:T(8,128)(2,1)S(1)}, u32[]{:S(2)}, u32[]{:S(2)}) collective-permute-start(bf16[128,2048]{1,0:T(8,128)(2,1)} %get-tuple-element.88), channel_id=1, source_target_pairs={{0,6},{2,0},{4,2},{6,4},{1,7},{3,1},{5,3},{7,5},{8,14},{10,8},{12,... | collective-permute-start | bytes 1572872 | tf_op jit(solution)/shard_map/ppermute | solution.py:36
  374.2 228.1 %reduce-scatter.9.cloned.1.call-start = ((), (), s32[]{:S(2)}) async-start(), calls=%async_computation.10 | async-start | bytes 3244032 | tf_op jit(solution)/shard_map/reduce_scatter | solution.py:213
  395.3 27.2 %collective-permute-start.27 = (bf16[128,2048]{1,0:T(8,128)(2,1)S(1)}, bf16[128,2048]{1,0:T(8,128)(2,1)S(1)}, u32[]{:S(2)}, u32[]{:S(2)}) collective-permute-start(bf16[128,2048]{1,0:T(8,128)(2,1)S(1)} %get-tuple-element.46), channel_id=1, source_target_pairs={{0,4},{2,6},{4,0},{6,2},{1,5},{3,7},{5,1},{7,3},{8,12},{10,14},{12... | collective-permute-start | bytes 1572872 | tf_op jit(solution)/shard_map/ppermute | solution.py:36
  396.1 26.4 %collective-permute-start.26 = (bf16[128,2048]{1,0:T(8,128)(2,1)S(1)}, bf16[128,2048]{1,0:T(8,128)(2,1)S(1)}, u32[]{:S(2)}, u32[]{:S(2)}) collective-permute-start(bf16[128,2048]{1,0:T(8,128)(2,1)S(1)} %get-tuple-element.46), channel_id=1, source_target_pairs={{0,6},{2,0},{4,2},{6,4},{1,7},{3,1},{5,3},{7,5},{8,14},{10,8},{12,... | collective-permute-start | bytes 1572872 | tf_op jit(solution)/shard_map/ppermute | solution.py:36
  399.8 52.3 %collective-permute-start.46 = (bf16[2048,704]{0,1:T(8,128)(2,1)S(1)}, bf16[2048,704]{0,1:T(8,128)(2,1)S(1)}, u32[]{:S(2)}, u32[]{:S(2)}) collective-permute-start(bf16[2048,704]{0,1:T(8,128)(2,1)S(1)} %convolution_convert_fusion.1), channel_id=1, source_target_pairs={{0,1},{1,0},{2,3},{3,2},{4,5},{5,4},{6,7},{7,6},{8,9},{9,8},{10,11... | collective-permute-start | bytes 8650760 | tf_op jit(solution)/shard_map/ppermute | solution.py:32
  406.9 72.5 %collective-permute-start.51 = (bf16[2048,704]{0,1:T(8,128)(2,1)}, bf16[2048,704]{0,1:T(8,128)(2,1)}, u32[]{:S(2)}, u32[]{:S(2)}) collective-permute-start(bf16[2048,704]{0,1:T(8,128)(2,1)} %convolution_convert_fusion), channel_id=1, source_target_pairs={{0,1},{1,0},{2,3},{3,2},{4,5},{5,4},{6,7},{7,6},{8,9},{9,8},{10,11... | collective-permute-start | bytes 8650760 | tf_op jit(solution)/shard_map/ppermute | solution.py:32
  408.5 95.5 %collective-permute-start.19 = (bf16[128,2048]{1,0:T(8,128)(2,1)}, bf16[128,2048]{1,0:T(8,128)(2,1)}, u32[]{:S(2)}, u32[]{:S(2)}) collective-permute-start(bf16[128,2048]{1,0:T(8,128)(2,1)} %get-tuple-element.127), channel_id=1, source_target_pairs={{0,1},{1,0},{2,3},{3,2},{4,5},{5,4},{6,7},{7,6},{8,9},{9,8},{10,11... | collective-permute-start | bytes 1572872 | tf_op jit(solution)/shard_map/ppermute | solution.py:32
  455.9 150.1 %reduce-scatter.11.cloned.1.call-start = ((), (), s32[]{:S(2)}) async-start(), calls=%async_computation.11 | async-start | bytes 3244032 | tf_op jit(solution)/shard_map/reduce_scatter | solution.py:213
  484.9 174.0 %reduce-scatter.5.cloned.1.call-start = ((), (), s32[]{:S(2)}) async-start(), calls=%async_computation.8 | async-start | bytes 2949120 | tf_op jit(solution)/shard_map/reduce_scatter | solution.py:213
  502.9 93.7 %collective-permute-start.35 = (bf16[2048,640]{0,1:T(8,128)(2,1)}, bf16[2048,640]{0,1:T(8,128)(2,1)}, u32[]{:S(2)}, u32[]{:S(2)}) collective-permute-start(bf16[2048,640]{0,1:T(8,128)(2,1)} %select_convert_fusion), channel_id=1, source_target_pairs={{0,1},{1,0},{2,3},{3,2},{4,5},{5,4},{6,7},{7,6},{8,9},{9,8},{10,11... | collective-permute-start | bytes 7864328 | tf_op jit(solution)/shard_map/ppermute | solution.py:32
  518.7 75.1 %collective-permute-start.34 = (bf16[128,2048]{1,0:T(8,128)(2,1)}, bf16[128,2048]{1,0:T(8,128)(2,1)}, u32[]{:S(2)}, u32[]{:S(2)}) collective-permute-start(bf16[128,2048]{1,0:T(8,128)(2,1)} %fusion.27), channel_id=1, source_target_pairs={{0,1},{1,0},{2,3},{3,2},{4,5},{5,4},{6,7},{7,6},{8,9},{9,8},{10,11... | collective-permute-start | bytes 1572872 | tf_op jit(solution)/shard_map/ppermute | solution.py:32
  606.0 27.0 %collective-permute-start.52 = (bf16[256,704]{0,1:T(8,128)(2,1)}, bf16[256,704]{0,1:T(8,128)(2,1)S(1)}, u32[]{:S(2)}, u32[]{:S(2)}) collective-permute-start(bf16[256,704]{0,1:T(8,128)(2,1)} %reduce-scatter.11.cloned.1.call-done), channel_id=1, source_target_pairs={{0,8},{8,0},{1,9},{9,1},{2,10},{10,2},{3,11},{11,3},{4,12},{12,4},... | collective-permute-start | bytes 1081352 | tf_op jit(solution)/shard_map/ppermute | solution.py:156
  607.2 26.8 %collective-permute-start.43 = (bf16[256,704]{0,1:T(8,128)(2,1)S(1)}, bf16[256,704]{0,1:T(8,128)(2,1)S(1)}, u32[]{:S(2)}, u32[]{:S(2)}) collective-permute-start(bf16[256,704]{0,1:T(8,128)(2,1)S(1)} %get-tuple-element.42), channel_id=1, source_target_pairs={{0,6},{2,0},{4,2},{6,4},{1,7},{3,1},{5,3},{7,5},{8,14},{10,8},{12,... | collective-permute-start | bytes 1081352 | tf_op jit(solution)/shard_map/ppermute | solution.py:36
  608.0 26.1 %collective-permute-start.44 = (bf16[256,704]{0,1:T(8,128)(2,1)S(1)}, bf16[256,704]{0,1:T(8,128)(2,1)S(1)}, u32[]{:S(2)}, u32[]{:S(2)}) collective-permute-start(bf16[256,704]{0,1:T(8,128)(2,1)S(1)} %get-tuple-element.42), channel_id=1, source_target_pairs={{0,4},{2,6},{4,0},{6,2},{1,5},{3,7},{5,1},{7,3},{8,12},{10,14},{12... | collective-permute-start | bytes 1081352 | tf_op jit(solution)/shard_map/ppermute | solution.py:36
  609.3 27.5 %collective-permute-start.45 = (bf16[256,704]{0,1:T(8,128)(2,1)S(1)}, bf16[256,704]{0,1:T(8,128)(2,1)S(1)}, u32[]{:S(2)}, u32[]{:S(2)}) collective-permute-start(bf16[256,704]{0,1:T(8,128)(2,1)S(1)} %get-tuple-element.42), channel_id=1, source_target_pairs={{0,2},{2,4},{4,6},{6,0},{1,3},{3,5},{5,7},{7,1},{8,10},{10,12},{12... | collective-permute-start | bytes 1081352 | tf_op jit(solution)/shard_map/ppermute | solution.py:36
  638.8 28.6 %collective-permute-start.55 = (bf16[256,704]{0,1:T(8,128)(2,1)}, bf16[256,704]{0,1:T(8,128)(2,1)}, u32[]{:S(2)}, u32[]{:S(2)}) collective-permute-start(bf16[256,704]{0,1:T(8,128)(2,1)} %get-tuple-element.38), channel_id=1, source_target_pairs={{0,2},{2,4},{4,6},{6,0},{1,3},{3,5},{5,7},{7,1},{8,10},{10,12},{12... | collective-permute-start | bytes 1081352 | tf_op jit(solution)/shard_map/ppermute | solution.py:36
  (126 other events, 1827.4 us)
Sparse Core Ops, SparseCore 0:
  21.6 46.7 all-gather.4
  70.6 56.2 all-gather.10
  129.0 51.5 all-gather.8
  182.6 51.3 all-gather.6
  374.4 41.6 reduce-scatter.6
  456.0 44.1 reduce-scatter.8
  503.2 44.1 reduce-scatter.10
  602.5 46.9 reduce-scatter.4
where the time goes:
time: 734 us; the launch traced here: 725 us
  waiting for transfers between devices  310 us (42%)
  matrix products  114 us (16%)
  starting transfers between devices  91.1 us (12%)
  blocking collectives  70.6 us (10%)
  local copies, waits for them, and re-layouts  64.2 us (9%)
  other arithmetic  58.3 us (8%)
  between operations  17 us (2%)
    ppermute x36, waiting for transfers between devices, shift_x(): return lax.ppermute(value, 'x', [(i, (i + hop) % 4) for i in range(4)])  148 us
    psum x1, blocking collectives, per_device(): lax.psum(jnp.stack([gain_attn_local, gain_ffn_local]), ('yl', 'z', 'yh',...  70.6 us
    all_gather x3, waiting for transfers between devices, hidden_units(): own = lax.all_gather(own, SHARD, axis=0, tiled=True)  70.4 us
    ppermute x6, waiting for transfers between devices, across_y(): return lax.ppermute(value, 'yh', SWAP)  46.1 us
    ppermute x13, starting transfers between devices, swap_cores(): return lax.ppermute(value, 'tp', SWAP)  43.7 us
    all_gather x1, waiting for transfers between devices, per_device(): pack = lax.all_gather(pack, SHARD, axis=0, tiled=True)  42.6 us
    ppermute x36, starting transfers between devices, shift_x(): return lax.ppermute(value, 'x', [(i, (i + hop) % 4) for i in range(4)])  40.2 us
    unnamed x222, local copies, waits for them, and re-layouts  38.6 us
  transfers between devices with their start and end apart: 64, of which 31 were waited for; matrix products, arithmetic and copies ran while one was open for 26% of the time, Pallas kernels for 0%

commit v1 on v0

--- a/solution.py
+++ b/solution.py
@@ -118,7 +118,9 @@
 
     def hidden_units(weight):
         own = half(lax.dynamic_slice_in_dim(weight, x_at * units, units, axis=1))
-        own = lax.all_gather(own, SHARD, axis=0, tiled=True)
+        own = jnp.concatenate(
+            lax.all_to_all(jnp.stack([own] * lax.axis_size(SHARD)), SHARD, 0, 0), axis=0
+        )
         return (own, swap_cores(own))
 
     xval = lax.dynamic_slice_in_dim(tokens[0], core * rows, rows, axis=0).astype(F32)

time: 734 us -> 694 us (0.946)
  waiting for transfers between devices: 310 us -> 238 us
  local copies, waits for them, and re-layouts: 64.2 us -> 82.6 us
    all_gather x3 -> x0, waiting for transfers between devices: 70.4 us -> none  [hidden_units(): own = lax.all_gather(own, SHARD, axis=0, tiled=True)]
    ppermute x36, waiting for transfers between devices: 148 us -> 113 us  [shift_x(): return lax.ppermute(value, 'x', [(i, (i + hop) % 4) for i in range(4)])]
    all_to_all x0 -> x3, waiting for transfers between devices: none -> 20.2 us  [hidden_units(): lax.all_to_all(jnp.stack([own] * lax.axis_size(SHARD)), SHARD, 0, 0)]
    all_to_all x0 -> x3, starting transfers between devices: none -> 18.4 us  [hidden_units(): lax.all_to_all(jnp.stack([own] * lax.axis_size(SHARD)), SHARD, 0, 0)]
    all_gather x1, waiting for transfers between devices: 42.6 us -> 58.1 us  [per_device(): pack = lax.all_gather(pack, SHARD, axis=0, tiled=True)]
    ppermute x36, starting transfers between devices: 40.2 us -> 30.7 us  [shift_x(): return lax.ppermute(value, 'x', [(i, (i + hop) % 4) for i in range(4)])]
    reshape x0 -> x3, local copies, waits for them, and re-layouts: none -> 8.1 us  [hidden_units(): jnp.concatenate(lax.all_to_all(jnp.stack([own] * lax.axis_size(SHARD)), S...]
    unnamed x222 -> x236, local copies, waits for them, and re-layouts: 38.6 us -> 39.9 us
  transfers between devices with their start and end apart: 64 -> 64, of which waited for: 31 -> 25; matrix products, arithmetic and copies ran while one was open for 26% -> 31% of each run, Pallas kernels for 0% -> 0%
where the time goes in v1:
time: 694 us; the launch traced here: 684 us
  waiting for transfers between devices  238 us (34%)
  matrix products  116 us (17%)
  starting transfers between devices  97.9 us (14%)
  local copies, waits for them, and re-layouts  82.6 us (12%)
  blocking collectives  72.2 us (10%)
  other arithmetic  60.6 us (9%)
  between operations  16.8 us (2%)
    ppermute x36, waiting for transfers between devices, shift_x(): return lax.ppermute(value, 'x', [(i, (i + hop) % 4) for i in range(4)])  113 us
    psum x1, blocking collectives, per_device(): lax.psum(jnp.stack([gain_attn_local, gain_ffn_local]), ('yl', 'z', 'yh',...  72.2 us
    all_gather x1, waiting for transfers between devices, per_device(): pack = lax.all_gather(pack, SHARD, axis=0, tiled=True)  58.1 us
    ppermute x13, starting transfers between devices, swap_cores(): return lax.ppermute(value, 'tp', SWAP)  41.5 us
    ppermute x6, waiting for transfers between devices, across_y(): return lax.ppermute(value, 'yh', SWAP)  41.3 us
    unnamed x236, local copies, waits for them, and re-layouts  39.9 us
    ppermute x36, starting transfers between devices, shift_x(): return lax.ppermute(value, 'x', [(i, (i + hop) % 4) for i in range(4)])  30.7 us
    dot_general x8, matrix products, mm_tn(): lax.dot_general(left, right, (((0,), (0,)), ((), ())), preferred_element_...  23.9 us
  transfers between devices with their start and end apart: 64, of which 25 were waited for; matrix products, arithmetic and copies ran while one was open for 31% of the time, Pallas kernels for 0%

profile of v1, /device:TPU:17, one launch (start us, length us, event | category | flops | bytes accessed | tf_op | source)
XLA Modules:
  0.0 684.2 jit_solution(18074132467418556018)
XLA Ops:
  35.7 5.9 all-to-all-start.2
  41.5 58.1 %all-gather.2.cloned.1.call-done = bf16[2048,640]{0,1:T(8,128)(2,1)} async-done(((bf16[256,640]{0,1:T(8,128)(2,1)}), bf16[2048,640]{0,1:T(8,128)(2,1)}) %all-gather.2.cloned.1.call-update) | async-done | bytes 2621456 | tf_op jit(solution)/shard_map/all_gather | solution.py:111
  120.9 6.2 collective-permute-done.5
  134.9 8.1 %all-to-all-start.1 = ((bf16[8,256,704]{1,2,0:T(8,128)(2,1)}), bf16[8,256,704]{1,2,0:T(8,128)(2,1)S(1)}, u32[]{:S(2)}, u32[]{:S(2)}) async-start(bf16[8,256,704]{1,2,0:T(8,128)(2,1)} %stack.135), calls=%async_computation.1 | async-start | bytes 5767168 | tf_op jit(solution)/shard_map/all_to_all | solution.py:122
  154.4 7.6 %select_reduce_fusion = (f32[4,512]{1,0:T(4,128)S(1)}, f32[4,512,2048]{2,1,0:T(8,128)}) fusion(pred[512,2048]{1,0:T(8,128)(4,1)S(1)} %copy-done.18, bf16[2048,256]{1,0:T(8,128)(2,1)S(1)} %pad_maximum_fusion.15, bf16[1,512,128]{2,1,0:T(8,128)(2,1)S(1)} %get-tuple-element.118, bf16[1,512,128]{2,1,0:T(8,128)(2,1)S(1)} %fusion.76, ...), kind=kOutput, calls=%fused_computation.3 | convolution fusion | flops 1087109120 | bytes 18882560 | tf_op jit(solution)/shard_map/htd,nd->htn/dot_general | solution.py:166
  162.0 8.4 %fusion.1 = f32[4,512]{1,0:T(4,128)S(1)} fusion(f32[4,512,2048]{2,1,0:T(8,128)} %get-tuple-element.186, f32[4,512]{1,0:T(4,128)S(1)} %get-tuple-element.185, pred[512,2048]{1,0:T(8,128)(4,1)S(1)} %copy-done.18), kind=kLoop, calls=%fused_computation.5 | loop fusion | flops 20969472 | bytes 17842176 | tf_op jit(solution)/shard_map/reduce_sum | solution.py:170
  170.4 7.3 %all-to-all-done.1 = bf16[8,256,704]{1,2,0:T(8,128)(2,1)S(1)} async-done(((bf16[8,256,704]{1,2,0:T(8,128)(2,1)}), bf16[8,256,704]{1,2,0:T(8,128)(2,1)S(1)}, u32[]{:S(2)}, u32[]{:S(2)}) %all-to-all-start.1) | async-done | bytes 2883616 | tf_op jit(solution)/shard_map/all_to_all | solution.py:122
  180.4 4.4 all-to-all-start
  184.9 9.4 %fusion.43 = (bf16[512,4,128]{0,2,1:T(8,128)(2,1)S(1)}, f32[4,512,128]{1,2,0:T(8,128)}) fusion(f32[512,4]{0,1:T(4,128)S(1)} %bitcast.261, bf16[2048,256]{1,0:T(8,128)(2,1)} %copy-done.39, f32[4,512,2048]{2,1,0:T(8,128)} %get-tuple-element.186, f32[4,512]{1,0:T(4,128)S(1)} %get-tuple-element.185, pred[512,2048]{1,0:T(8,128)(4,1)} %compare_and_fusion), kind=kOutput, calls=%fused_computation.100 | convolution fusion | flops 1095237632 | bytes 19939328 | tf_op jit(solution)/shard_map/htn,nd->htd/dot_general | solution.py:171
  206.5 12.9 %all-to-all-done = bf16[8,256,704]{1,2,0:T(8,128)(2,1)} async-done(((bf16[8,256,704]{1,2,0:T(8,128)(2,1)}), bf16[8,256,704]{1,2,0:T(8,128)(2,1)}, u32[]{:S(2)}, u32[]{:S(2)}) %all-to-all-start) | async-done | bytes 2883616 | tf_op jit(solution)/shard_map/all_to_all | solution.py:122
  230.5 7.1 %collective-permute-done.22 = bf16[128,2048]{1,0:T(8,128)(2,1)} collective-permute-done((bf16[128,2048]{1,0:T(8,128)(2,1)}, bf16[128,2048]{1,0:T(8,128)(2,1)}, u32[]{:S(2)}, u32[]{:S(2)}) %collective-permute-start.22) | collective-permute-done | bytes 524320 | tf_op jit(solution)/shard_map/ppermute | solution.py:36
  237.6 11.6 %collective-permute-start.13 = (bf16[2048,704]{0,1:T(8,128)(2,1)S(1)}, bf16[2048,704]{0,1:T(8,128)(2,1)S(1)}, u32[]{:S(2)}, u32[]{:S(2)}) collective-permute-start(bf16[2048,704]{0,1:T(8,128)(2,1)S(1)} %bitcast.254), channel_id=1, source_target_pairs={{0,1},{1,0},{2,3},{3,2},{4,5},{5,4},{6,7},{7,6},{8,9},{9,8},{10,11... | collective-permute-start | bytes 8650760 | tf_op jit(solution)/shard_map/ppermute | solution.py:32
  256.3 19.3 %collective-permute-done.12 = bf16[128,2048]{1,0:T(8,128)(2,1)S(1)} collective-permute-done((bf16[128,2048]{1,0:T(8,128)(2,1)S(1)}, bf16[128,2048]{1,0:T(8,128)(2,1)S(1)}, u32[]{:S(2)}, u32[]{:S(2)}) %collective-permute-start.12) | collective-permute-done | bytes 524320 | tf_op jit(solution)/shard_map/ppermute | solution.py:36
  307.2 5.7 fusion.130
  315.6 8.9 %collective-permute-done.25 = bf16[128,2048]{1,0:T(8,128)(2,1)S(1)} collective-permute-done((bf16[128,2048]{1,0:T(8,128)(2,1)S(1)}, bf16[128,2048]{1,0:T(8,128)(2,1)S(1)}, u32[]{:S(2)}, u32[]{:S(2)}) %collective-permute-start.25) | collective-permute-done | bytes 524320 | tf_op jit(solution)/shard_map/ppermute | solution.py:36
  333.4 13.9 %collective-permute-done.18 = bf16[128,2048]{1,0:T(8,128)(2,1)} collective-permute-done((bf16[128,2048]{1,0:T(8,128)(2,1)}, bf16[128,2048]{1,0:T(8,128)(2,1)}, u32[]{:S(2)}, u32[]{:S(2)}) %collective-permute-start.18) | collective-permute-done | bytes 524320 | tf_op jit(solution)/shard_map/ppermute | solution.py:36
  347.3 4.5 collective-permute-done.16
  362.9 4.5 convolution_convert_fusion
  369.4 13.5 %collective-permute-start.19 = (bf16[128,2048]{1,0:T(8,128)(2,1)}, bf16[128,2048]{1,0:T(8,128)(2,1)}, u32[]{:S(2)}, u32[]{:S(2)}) collective-permute-start(bf16[128,2048]{1,0:T(8,128)(2,1)} %get-tuple-element.149), channel_id=1, source_target_pairs={{0,1},{1,0},{2,3},{3,2},{4,5},{5,4},{6,7},{7,6},{8,9},{9,8},{10,11... | collective-permute-start | bytes 1572872 | tf_op jit(solution)/shard_map/ppermute | solution.py:32
  384.8 12.4 %multiply_convert_fusion = bf16[4,512,2048]{2,1,0:T(8,128)(2,1)} fusion(f32[4,512,2048]{2,1,0:T(8,128)} %get-tuple-element.186, f32[4,512]{1,0:T(4,128)S(1)} %get-tuple-element.193, f32[4,512]{1,0:T(4,128)S(1)} %log_add_fusion, pred[512,2048]{1,0:T(8,128)(4,1)S(1)} %copy-done.19, bf16[4,512,128]{1,2,0:T(8,128)(2,1)S(1)} %bitcast.259, ...), kind=kOutput, calls=%fused_computation | convolution fusion | flops 1103101952 | bytes 27279360 | tf_op jit(solution)/shard_map/htd,nd->htn/dot_general | solution.py:233
  397.2 5.8 convolution_bitcast_fusion
  403.0 8.1 %fusion.9 = f32[2048,128]{1,0:T(8,128)S(1)} fusion(bf16[4,512,128]{1,2,0:T(8,128)(2,1)S(1)} %bitcast.260, f32[4,512,2048]{2,1,0:T(8,128)} %get-tuple-element.186, f32[4,512]{1,0:T(4,128)S(1)} %log_add_fusion, pred[512,2048]{1,0:T(8,128)(4,1)S(1)} %copy-done.19), kind=kOutput, calls=%fused_computation.33 | convolution fusion | flops 1090519040 | bytes 19406848 | tf_op jit(solution)/shard_map/htn,htd->nd/dot_general | solution.py:237
  425.0 11.4 %collective-permute-done.30 = bf16[512,256]{1,0:T(8,128)(2,1)S(1)} collective-permute-done((bf16[512,256]{1,0:T(8,128)(2,1)S(1)}, bf16[512,256]{1,0:T(8,128)(2,1)S(1)}, u32[]{:S(2)}, u32[]{:S(2)}) %collective-permute-start.30) | collective-permute-done | bytes 262176 | tf_op jit(solution)/shard_map/ppermute | solution.py:158
  439.0 5.5 add_convert_fusion
  462.7 11.0 %collective-permute-done.32 = bf16[128,2048]{1,0:T(8,128)(2,1)S(1)} collective-permute-done((bf16[128,2048]{1,0:T(8,128)(2,1)S(1)}, bf16[128,2048]{1,0:T(8,128)(2,1)S(1)}, u32[]{:S(2)}, u32[]{:S(2)}) %collective-permute-start.32) | collective-permute-done | bytes 524320 | tf_op jit(solution)/shard_map/ppermute | solution.py:36
  479.3 72.2 %psum.7 = f32[2,2048]{1,0:T(2,128)S(1)} all-reduce(f32[2,2048]{1,0:T(2,128)S(1)} %pad_maximum_fusion.34), channel_id=1, replica_groups=mesh['yl'=2,'z'=4,'yh'=2,'x'=4,'tp'=2] {'yl','z','yh','x','tp'}, use_global_device_ids=true, to_apply=%region_9.10 | all-reduce | flops 4096 | bytes 32768 | tf_op jit(solution)/shard_map/psum | solution.py:266
  555.2 5.8 add_convert_fusion.3
  568.0 8.9 %collective-permute-done.47 = bf16[256,704]{0,1:T(8,128)(2,1)S(1)} collective-permute-done((bf16[256,704]{0,1:T(8,128)(2,1)}, bf16[256,704]{0,1:T(8,128)(2,1)S(1)}, u32[]{:S(2)}, u32[]{:S(2)}) %collective-permute-start.47) | collective-permute-done | bytes 360480 | tf_op jit(solution)/shard_map/ppermute | solution.py:158
  577.1 14.8 %collective-permute-done.52 = bf16[256,704]{0,1:T(8,128)(2,1)S(1)} collective-permute-done((bf16[256,704]{0,1:T(8,128)(2,1)}, bf16[256,704]{0,1:T(8,128)(2,1)S(1)}, u32[]{:S(2)}, u32[]{:S(2)}) %collective-permute-start.52) | collective-permute-done | bytes 360480 | tf_op jit(solution)/shard_map/ppermute | solution.py:158
  600.3 14.6 %collective-permute-done.50 = bf16[256,704]{0,1:T(8,128)(2,1)S(1)} collective-permute-done((bf16[256,704]{0,1:T(8,128)(2,1)S(1)}, bf16[256,704]{0,1:T(8,128)(2,1)S(1)}, u32[]{:S(2)}, u32[]{:S(2)}) %collective-permute-start.50) | collective-permute-done | bytes 360480 | tf_op jit(solution)/shard_map/ppermute | solution.py:36
  619.5 7.5 %collective-permute-done.55 = bf16[256,704]{0,1:T(8,128)(2,1)} collective-permute-done((bf16[256,704]{0,1:T(8,128)(2,1)}, bf16[256,704]{0,1:T(8,128)(2,1)}, u32[]{:S(2)}, u32[]{:S(2)}) %collective-permute-start.55) | collective-permute-done | bytes 360480 | tf_op jit(solution)/shard_map/ppermute | solution.py:36
  640.6 9.2 %collective-permute-done.39 = bf16[256,640]{0,1:T(8,128)(2,1)S(1)} collective-permute-done((bf16[256,640]{0,1:T(8,128)(2,1)S(1)}, bf16[256,640]{0,1:T(8,128)(2,1)S(1)}, u32[]{:S(2)}, u32[]{:S(2)}) %collective-permute-start.39) | collective-permute-done | bytes 327712 | tf_op jit(solution)/shard_map/ppermute | solution.py:36
  (494 shorter events, 262.9 us)
Async XLA Ops:
  7.2 92.5 %all-gather.2.cloned.1.call-start = ((), (), s32[]{:S(2)}) async-start(), calls=%async_computation.7 | async-start | bytes 2949120 | tf_op jit(solution)/shard_map/all_gather | solution.py:111
  25.3 85.9 %collective-permute-start.2 = (bf16[128,2048]{1,0:T(8,128)(2,1)}, bf16[128,2048]{1,0:T(8,128)(2,1)}, u32[]{:S(2)}, u32[]{:S(2)}) collective-permute-start(bf16[128,2048]{1,0:T(8,128)(2,1)} %fusion.23), channel_id=1, source_target_pairs={{0,2},{2,4},{4,6},{6,0},{1,3},{3,5},{5,7},{7,1},{8,10},{10,12},{12... | collective-permute-start | bytes 1572872 | tf_op jit(solution)/shard_map/ppermute | solution.py:36
  26.5 84.7 %collective-permute-start.1 = (bf16[128,2048]{1,0:T(8,128)(2,1)}, bf16[128,2048]{1,0:T(8,128)(2,1)}, u32[]{:S(2)}, u32[]{:S(2)}) collective-permute-start(bf16[128,2048]{1,0:T(8,128)(2,1)} %fusion.23), channel_id=1, source_target_pairs={{0,4},{2,6},{4,0},{6,2},{1,5},{3,7},{5,1},{7,3},{8,12},{10,14},{12... | collective-permute-start | bytes 1572872 | tf_op jit(solution)/shard_map/ppermute | solution.py:36
  28.3 82.9 %collective-permute-start = (bf16[128,2048]{1,0:T(8,128)(2,1)}, bf16[128,2048]{1,0:T(8,128)(2,1)}, u32[]{:S(2)}, u32[]{:S(2)}) collective-permute-start(bf16[128,2048]{1,0:T(8,128)(2,1)} %fusion.23), channel_id=1, source_target_pairs={{0,6},{2,0},{4,2},{6,4},{1,7},{3,1},{5,3},{7,5},{8,14},{10,8},{12,... | collective-permute-start | bytes 1572872 | tf_op jit(solution)/shard_map/ppermute | solution.py:36
  35.7 97.5 %all-to-all-start.2 = ((bf16[8,256,704]{1,2,0:T(8,128)(2,1)}), bf16[8,256,704]{1,2,0:T(8,128)(2,1)}, u32[]{:S(2)}, u32[]{:S(2)}) async-start(bf16[8,256,704]{1,2,0:T(8,128)(2,1)} %stack.136), calls=%async_computation.2 | async-start | bytes 5767168 | tf_op jit(solution)/shard_map/all_to_all | solution.py:122
  134.9 42.7 %all-to-all-start.1 = ((bf16[8,256,704]{1,2,0:T(8,128)(2,1)}), bf16[8,256,704]{1,2,0:T(8,128)(2,1)S(1)}, u32[]{:S(2)}, u32[]{:S(2)}) async-start(bf16[8,256,704]{1,2,0:T(8,128)(2,1)} %stack.135), calls=%async_computation.1 | async-start | bytes 5767168 | tf_op jit(solution)/shard_map/all_to_all | solution.py:122
  146.8 103.3 %collective-permute-start.15 = (bf16[2048,704]{0,1:T(8,128)(2,1)}, bf16[2048,704]{0,1:T(8,128)(2,1)}, u32[]{:S(2)}, u32[]{:S(2)}) collective-permute-start(bf16[2048,704]{0,1:T(8,128)(2,1)} %bitcast.96), channel_id=1, source_target_pairs={{0,1},{1,0},{2,3},{3,2},{4,5},{5,4},{6,7},{7,6},{8,9},{9,8},{10,11... | collective-permute-start | bytes 8650760 | tf_op jit(solution)/shard_map/ppermute | solution.py:32
  180.4 39.0 %all-to-all-start = ((bf16[8,256,704]{1,2,0:T(8,128)(2,1)}), bf16[8,256,704]{1,2,0:T(8,128)(2,1)}, u32[]{:S(2)}, u32[]{:S(2)}) async-start(bf16[8,256,704]{1,2,0:T(8,128)(2,1)} %stack.134), calls=%async_computation | async-start | bytes 5767168 | tf_op jit(solution)/shard_map/all_to_all | solution.py:122
  184.8 369.6 %reduce-scatter.7.cloned.1.call-start = ((), (), s32[]{:S(2)}) async-start(), calls=%async_computation.9 | async-start | bytes 3244032 | tf_op jit(solution)/shard_map/reduce_scatter | solution.py:215
  202.8 34.9 %collective-permute-start.22 = (bf16[128,2048]{1,0:T(8,128)(2,1)}, bf16[128,2048]{1,0:T(8,128)(2,1)}, u32[]{:S(2)}, u32[]{:S(2)}) collective-permute-start(bf16[128,2048]{1,0:T(8,128)(2,1)} %fusion.20), channel_id=1, source_target_pairs={{0,2},{2,4},{4,6},{6,0},{1,3},{3,5},{5,7},{7,1},{8,10},{10,12},{12... | collective-permute-start | bytes 1572872 | tf_op jit(solution)/shard_map/ppermute | solution.py:36
  221.8 27.4 %collective-permute-start.21 = (bf16[128,2048]{1,0:T(8,128)(2,1)}, bf16[128,2048]{1,0:T(8,128)(2,1)S(1)}, u32[]{:S(2)}, u32[]{:S(2)}) collective-permute-start(bf16[128,2048]{1,0:T(8,128)(2,1)} %fusion.20), channel_id=1, source_target_pairs={{0,4},{2,6},{4,0},{6,2},{1,5},{3,7},{5,1},{7,3},{8,12},{10,14},{12... | collective-permute-start | bytes 1572872 | tf_op jit(solution)/shard_map/ppermute | solution.py:36
  224.0 63.4 %collective-permute-start.14 = (bf16[2048,704]{0,1:T(8,128)(2,1)S(1)}, bf16[2048,704]{0,1:T(8,128)(2,1)S(1)}, u32[]{:S(2)}, u32[]{:S(2)}) collective-permute-start(bf16[2048,704]{0,1:T(8,128)(2,1)S(1)} %bitcast.251), channel_id=1, source_target_pairs={{0,1},{1,0},{2,3},{3,2},{4,5},{5,4},{6,7},{7,6},{8,9},{9,8},{10,11... | collective-permute-start | bytes 8650760 | tf_op jit(solution)/shard_map/ppermute | solution.py:32
  237.6 51.5 %collective-permute-start.13 = (bf16[2048,704]{0,1:T(8,128)(2,1)S(1)}, bf16[2048,704]{0,1:T(8,128)(2,1)S(1)}, u32[]{:S(2)}, u32[]{:S(2)}) collective-permute-start(bf16[2048,704]{0,1:T(8,128)(2,1)S(1)} %bitcast.254), channel_id=1, source_target_pairs={{0,1},{1,0},{2,3},{3,2},{4,5},{5,4},{6,7},{7,6},{8,9},{9,8},{10,11... | collective-permute-start | bytes 8650760 | tf_op jit(solution)/shard_map/ppermute | solution.py:32
  249.2 26.3 %collective-permute-start.12 = (bf16[128,2048]{1,0:T(8,128)(2,1)S(1)}, bf16[128,2048]{1,0:T(8,128)(2,1)S(1)}, u32[]{:S(2)}, u32[]{:S(2)}) collective-permute-start(bf16[128,2048]{1,0:T(8,128)(2,1)S(1)} %multiply_convert_fusion.8), channel_id=1, source_target_pairs={{0,2},{2,4},{4,6},{6,0},{1,3},{3,5},{5,7},{7,1},{8,10},{10,12},{12... | collective-permute-start | bytes 1572872 | tf_op jit(solution)/shard_map/ppermute | solution.py:36
  294.6 35.7 %collective-permute-start.41 = (bf16[2048,704]{0,1:T(8,128)(2,1)S(1)}, bf16[2048,704]{0,1:T(8,128)(2,1)S(1)}, u32[]{:S(2)}, u32[]{:S(2)}) collective-permute-start(bf16[2048,704]{0,1:T(8,128)(2,1)S(1)} %convolution_convert_fusion.2), channel_id=1, source_target_pairs={{0,1},{1,0},{2,3},{3,2},{4,5},{5,4},{6,7},{7,6},{8,9},{9,8},{10,11... | collective-permute-start | bytes 8650760 | tf_op jit(solution)/shard_map/ppermute | solution.py:32
  302.3 27.4 %collective-permute-start.23 = (bf16[128,2048]{1,0:T(8,128)(2,1)S(1)}, bf16[128,2048]{1,0:T(8,128)(2,1)S(1)}, u32[]{:S(2)}, u32[]{:S(2)}) collective-permute-start(bf16[128,2048]{1,0:T(8,128)(2,1)S(1)} %get-tuple-element.106), channel_id=1, source_target_pairs={{0,4},{2,6},{4,0},{6,2},{1,5},{3,7},{5,1},{7,3},{8,12},{10,14},{12... | collective-permute-start | bytes 1572872 | tf_op jit(solution)/shard_map/ppermute | solution.py:36
  314.2 33.1 %collective-permute-start.18 = (bf16[128,2048]{1,0:T(8,128)(2,1)}, bf16[128,2048]{1,0:T(8,128)(2,1)}, u32[]{:S(2)}, u32[]{:S(2)}) collective-permute-start(bf16[128,2048]{1,0:T(8,128)(2,1)} %get-tuple-element.110), channel_id=1, source_target_pairs={{0,6},{2,0},{4,2},{6,4},{1,7},{3,1},{5,3},{7,5},{8,14},{10,8},{12,... | collective-permute-start | bytes 1572872 | tf_op jit(solution)/shard_map/ppermute | solution.py:36
  333.3 227.7 %reduce-scatter.9.cloned.1.call-start = ((), (), s32[]{:S(2)}) async-start(), calls=%async_computation.10 | async-start | bytes 3244032 | tf_op jit(solution)/shard_map/reduce_scatter | solution.py:215
  355.7 27.2 %collective-permute-start.27 = (bf16[128,2048]{1,0:T(8,128)(2,1)S(1)}, bf16[128,2048]{1,0:T(8,128)(2,1)S(1)}, u32[]{:S(2)}, u32[]{:S(2)}) collective-permute-start(bf16[128,2048]{1,0:T(8,128)(2,1)S(1)} %get-tuple-element.68), channel_id=1, source_target_pairs={{0,4},{2,6},{4,0},{6,2},{1,5},{3,7},{5,1},{7,3},{8,12},{10,14},{12... | collective-permute-start | bytes 1572872 | tf_op jit(solution)/shard_map/ppermute | solution.py:36
  356.0 26.9 %collective-permute-start.26 = (bf16[128,2048]{1,0:T(8,128)(2,1)S(1)}, bf16[128,2048]{1,0:T(8,128)(2,1)S(1)}, u32[]{:S(2)}, u32[]{:S(2)}) collective-permute-start(bf16[128,2048]{1,0:T(8,128)(2,1)S(1)} %get-tuple-element.68), channel_id=1, source_target_pairs={{0,6},{2,0},{4,2},{6,4},{1,7},{3,1},{5,3},{7,5},{8,14},{10,8},{12,... | collective-permute-start | bytes 1572872 | tf_op jit(solution)/shard_map/ppermute | solution.py:36
  360.1 51.2 %collective-permute-start.46 = (bf16[2048,704]{0,1:T(8,128)(2,1)S(1)}, bf16[2048,704]{0,1:T(8,128)(2,1)S(1)}, u32[]{:S(2)}, u32[]{:S(2)}) collective-permute-start(bf16[2048,704]{0,1:T(8,128)(2,1)S(1)} %convolution_convert_fusion.1), channel_id=1, source_target_pairs={{0,1},{1,0},{2,3},{3,2},{4,5},{5,4},{6,7},{7,6},{8,9},{9,8},{10,11... | collective-permute-start | bytes 8650760 | tf_op jit(solution)/shard_map/ppermute | solution.py:32
  367.3 71.3 %collective-permute-start.51 = (bf16[2048,704]{0,1:T(8,128)(2,1)}, bf16[2048,704]{0,1:T(8,128)(2,1)}, u32[]{:S(2)}, u32[]{:S(2)}) collective-permute-start(bf16[2048,704]{0,1:T(8,128)(2,1)} %convolution_convert_fusion), channel_id=1, source_target_pairs={{0,1},{1,0},{2,3},{3,2},{4,5},{5,4},{6,7},{7,6},{8,9},{9,8},{10,11... | collective-permute-start | bytes 8650760 | tf_op jit(solution)/shard_map/ppermute | solution.py:32
  369.4 92.1 %collective-permute-start.19 = (bf16[128,2048]{1,0:T(8,128)(2,1)}, bf16[128,2048]{1,0:T(8,128)(2,1)}, u32[]{:S(2)}, u32[]{:S(2)}) collective-permute-start(bf16[128,2048]{1,0:T(8,128)(2,1)} %get-tuple-element.149), channel_id=1, source_target_pairs={{0,1},{1,0},{2,3},{3,2},{4,5},{5,4},{6,7},{7,6},{8,9},{9,8},{10,11... | collective-permute-start | bytes 1572872 | tf_op jit(solution)/shard_map/ppermute | solution.py:32
  415.6 148.8 %reduce-scatter.11.cloned.1.call-start = ((), (), s32[]{:S(2)}) async-start(), calls=%async_computation.11 | async-start | bytes 3244032 | tf_op jit(solution)/shard_map/reduce_scatter | solution.py:215
  444.5 174.2 %reduce-scatter.5.cloned.1.call-start = ((), (), s32[]{:S(2)}) async-start(), calls=%async_computation.8 | async-start | bytes 2949120 | tf_op jit(solution)/shard_map/reduce_scatter | solution.py:215
  459.8 95.4 %collective-permute-start.35 = (bf16[2048,640]{0,1:T(8,128)(2,1)}, bf16[2048,640]{0,1:T(8,128)(2,1)}, u32[]{:S(2)}, u32[]{:S(2)}) collective-permute-start(bf16[2048,640]{0,1:T(8,128)(2,1)} %select_convert_fusion), channel_id=1, source_target_pairs={{0,1},{1,0},{2,3},{3,2},{4,5},{5,4},{6,7},{7,6},{8,9},{9,8},{10,11... | collective-permute-start | bytes 7864328 | tf_op jit(solution)/shard_map/ppermute | solution.py:32
  475.8 76.3 %collective-permute-start.34 = (bf16[128,2048]{1,0:T(8,128)(2,1)}, bf16[128,2048]{1,0:T(8,128)(2,1)}, u32[]{:S(2)}, u32[]{:S(2)}) collective-permute-start(bf16[128,2048]{1,0:T(8,128)(2,1)} %fusion.27), channel_id=1, source_target_pairs={{0,1},{1,0},{2,3},{3,2},{4,5},{5,4},{6,7},{7,6},{8,9},{9,8},{10,11... | collective-permute-start | bytes 1572872 | tf_op jit(solution)/shard_map/ppermute | solution.py:32
  564.4 27.6 %collective-permute-start.52 = (bf16[256,704]{0,1:T(8,128)(2,1)}, bf16[256,704]{0,1:T(8,128)(2,1)S(1)}, u32[]{:S(2)}, u32[]{:S(2)}) collective-permute-start(bf16[256,704]{0,1:T(8,128)(2,1)} %reduce-scatter.11.cloned.1.call-done), channel_id=1, source_target_pairs={{0,8},{8,0},{1,9},{9,1},{2,10},{10,2},{3,11},{11,3},{4,12},{12,4},... | collective-permute-start | bytes 1081352 | tf_op jit(solution)/shard_map/ppermute | solution.py:158
  565.5 27.4 %collective-permute-start.43 = (bf16[256,704]{0,1:T(8,128)(2,1)S(1)}, bf16[256,704]{0,1:T(8,128)(2,1)S(1)}, u32[]{:S(2)}, u32[]{:S(2)}) collective-permute-start(bf16[256,704]{0,1:T(8,128)(2,1)S(1)} %get-tuple-element.64), channel_id=1, source_target_pairs={{0,6},{2,0},{4,2},{6,4},{1,7},{3,1},{5,3},{7,5},{8,14},{10,8},{12,... | collective-permute-start | bytes 1081352 | tf_op jit(solution)/shard_map/ppermute | solution.py:36
  566.3 26.6 %collective-permute-start.44 = (bf16[256,704]{0,1:T(8,128)(2,1)S(1)}, bf16[256,704]{0,1:T(8,128)(2,1)S(1)}, u32[]{:S(2)}, u32[]{:S(2)}) collective-permute-start(bf16[256,704]{0,1:T(8,128)(2,1)S(1)} %get-tuple-element.64), channel_id=1, source_target_pairs={{0,4},{2,6},{4,0},{6,2},{1,5},{3,7},{5,1},{7,3},{8,12},{10,14},{12... | collective-permute-start | bytes 1081352 | tf_op jit(solution)/shard_map/ppermute | solution.py:36
  567.2 28.5 %collective-permute-start.45 = (bf16[256,704]{0,1:T(8,128)(2,1)S(1)}, bf16[256,704]{0,1:T(8,128)(2,1)S(1)}, u32[]{:S(2)}, u32[]{:S(2)}) collective-permute-start(bf16[256,704]{0,1:T(8,128)(2,1)S(1)} %get-tuple-element.64), channel_id=1, source_target_pairs={{0,2},{2,4},{4,6},{6,0},{1,3},{3,5},{5,7},{7,1},{8,10},{10,12},{12... | collective-permute-start | bytes 1081352 | tf_op jit(solution)/shard_map/ppermute | solution.py:36
  597.7 29.3 %collective-permute-start.55 = (bf16[256,704]{0,1:T(8,128)(2,1)}, bf16[256,704]{0,1:T(8,128)(2,1)}, u32[]{:S(2)}, u32[]{:S(2)}) collective-permute-start(bf16[256,704]{0,1:T(8,128)(2,1)} %get-tuple-element.60), channel_id=1, source_target_pairs={{0,2},{2,4},{4,6},{6,0},{1,3},{3,5},{5,7},{7,1},{8,10},{10,12},{12... | collective-permute-start | bytes 1081352 | tf_op jit(solution)/shard_map/ppermute | solution.py:36
  (133 other events, 1844.3 us)
Sparse Core Ops, SparseCore 0:
  21.6 77.9 all-gather.1
  333.4 41.7 reduce-scatter.6
  415.7 45.5 reduce-scatter.8
  464.1 42.0 reduce-scatter.10
  561.1 46.9 reduce-scatter.4
